TPU v7x, 512 devices: a whole 4x4x16 slice. The times are simulated.
512 devices in a mesh: req: 64 (over z, y), tensor: 8 (over x, core).
Axes of the slice: x: 4, y: 4, z: 16, core: 2. Of those that a mesh axis runs over, the one named last changes fastest.
Arguments:
- tokens: bfloat16 [16384, 2048], P('req', 'tensor'), may hold values from -6 to 6
- segment_ids: int32 [16384], P('req'), may hold values from 0 to 42, as said below
- prefix_lengths: int32 [43], replicated, may hold values from 0 to 256, as said below
- page_owner: int32 [4096, 1], P('req'), may hold values from 0 to 63; in each aligned block of 64 rows (0 to 63, 64 to 127, ...) at most 2 rows name the same one
- slot_perm: int32 [64, 128], P('req'), may hold values from 0 to 127, each once within a row
- ln_gain: float32 [2048], replicated, may hold values from 0.1 to 1.9
- ln_bias: float32 [2048], replicated, may hold values from -3 to 3
- qkv_weight: bfloat16 [2048, 3, 2048], P('req', None, 'tensor')
- qkv_bias: float32 [3, 2048], P(None, 'tensor'), may hold values from -3 to 3
- dense_weight: bfloat16 [2048, 2048], P('tensor', 'req'), may hold values from -0.375 to 0.375
- dense_bias: float32 [2048], P('tensor'), may hold values from -3 to 3
- fc1_weight: bfloat16 [2048, 4096], P('req', 'tensor'), may hold values from -0.125 to 0.125
- fc1_bias: float32 [4096], P('tensor'), may hold values from -3 to 3
- fc2_weight: bfloat16 [4096, 2048], P('tensor', 'req'), may hold values from -0.25 to 0.25
- fc2_bias: float32 [2048], P('tensor'), may hold values from -3 to 3
- prefix_cache: bfloat16 [16384, 2, 2048], P('req', None, 'tensor'), may hold values from -9 to 9
- cache_pool: bfloat16 [32768, 2, 2048], P('req', None, 'tensor'), may hold values from -6 to 6
Outputs:
- layer_out: bfloat16 [16384, 2048], P('req', 'tensor')
- new_pool: bfloat16 [32768, 2, 2048], P('req', None, 'tensor')
Inputs may be any that keep to these rules, and one draw needn't show every extreme that they name: `segment_ids`: labels 1 to 42 appear in order, each as one run of 257 to 512 rows, together filling all rows before the padding; segment 1 is 512 rows long; the last 128 rows are 0. `prefix_lengths`: entry 0 is 0 and entry 1 is 256. `page_owner`: among the pages of one index of req no owner appears more than 2 times, and some owner appears exactly 2 times. `slot_perm`: each row is a permutation of 0 to 127.
All inputs are finite; a program needn't handle non-finite values.
Results may differ from a plain program's by a relative error of at most 0.006.
The roundings to bfloat16 on the way count: a program that leaves them out, or rounds other values in their place, can miss the bound.
Values may be sent and summed in bfloat16 or wider, within the bound.
A program may use at most 64 MiB of HBM per device.

v0:
```python
import jax
import jax.numpy as jnp
from jax import lax
from jax.sharding import PartitionSpec as P

HEAD_DIM = 64
ROT = 32
SPAN = 2
SINKS = 4
PAGE = 4
WINDOW = 512
EPSILON = 1e-05


def from_behind(value, axis, steps):
    count = lax.axis_size(axis)
    leading, last = (max(0, -steps), min(count, count - steps))
    return lax.ppermute(value, axis, [(source, source + steps) for source in range(leading, last)])


def norm_rows(widened, gain, offset_bias):
    average = jnp.mean(widened, axis=-1, keepdims=True)
    centred = widened - average
    spread = jnp.mean(centred * centred, axis=-1, keepdims=True)
    return (centred * lax.rsqrt(spread + EPSILON) * gain + offset_bias).astype(jnp.bfloat16)


def label_rows(places, starts, prefix_lengths):
    labels = jnp.arange(starts.shape[0], dtype=jnp.int32)
    passed = (starts[None, :] <= places[:, None]) & (labels[None, :] >= 1)
    counted = jnp.sum(passed.astype(jnp.int32), axis=1)
    segment = jnp.where(places >= starts[0], 0, counted)
    segment = jnp.where(places < 0, -2, segment)
    onehot = segment[:, None] == labels[None, :]
    earliest = jnp.sum(jnp.where(onehot, starts[None, :], 0), axis=1)
    offset = jnp.sum(jnp.where(onehot, prefix_lengths[None, :], 0), axis=1)
    return (segment, offset + places - earliest)


def prefix_rows(block_id, rows_dev, prefix_count, starts, prefix_lengths):
    labels = jnp.arange(starts.shape[0], dtype=jnp.int32)
    located = (starts >= block_id * rows_dev) & (starts < (block_id + 1) * rows_dev) & (labels >= 1)
    owner_label = jnp.sum(jnp.where(located, labels, 0))
    length = jnp.sum(jnp.where(located, prefix_lengths, 0))
    places = jnp.arange(prefix_count, dtype=jnp.int32)
    usable = jnp.any(located) & (places < length)
    return (jnp.where(usable, owner_label, -2), places)


def rotate_heads(values, position):
    half_rot = ROT // 2
    frequency = 10000.0 ** (-2.0 * jnp.arange(half_rot, dtype=jnp.float32) / ROT)
    angles = position.astype(jnp.float32)[:, None] * frequency[None, :]
    cosine = jnp.cos(angles)[:, None, :]
    sine_vals = jnp.sin(angles)[:, None, :]
    lower = values[..., :half_rot]
    upper = values[..., half_rot:ROT]
    return jnp.concatenate(
        [lower * cosine - upper * sine_vals, upper * cosine + lower * sine_vals, values[..., ROT:]],
        axis=-1,
    )


def head_attention(query_rows, key_rows, value_rows, allowed):
    head_count = query_rows.shape[1] // HEAD_DIM
    score_scale = HEAD_DIM ** (-0.5)

    def one_head(head_index):
        query_cols = lax.dynamic_slice_in_dim(query_rows, head_index * HEAD_DIM, HEAD_DIM, 1)
        key_cols = lax.dynamic_slice_in_dim(key_rows, head_index * HEAD_DIM, HEAD_DIM, 1)
        value_cols = lax.dynamic_slice_in_dim(value_rows, head_index * HEAD_DIM, HEAD_DIM, 1)
        scores = (
            lax.dot_general(
                query_cols, key_cols, (((1,), (1,)), ((), ())), preferred_element_type=jnp.float32
            )
            * score_scale
        )
        masked = jnp.where(allowed, scores, -1e30)
        highest = jnp.max(masked, axis=1, keepdims=True)
        expo = jnp.where(allowed, jnp.exp(masked - highest), 0.0)
        denom = jnp.sum(expo, axis=1, keepdims=True)
        mixed = (
            jnp.dot(expo.astype(jnp.bfloat16), value_cols, preferred_element_type=jnp.float32)
            / denom
        )
        return mixed.astype(jnp.bfloat16)

    outcome = lax.map(one_head, jnp.arange(head_count, dtype=jnp.int32))
    return jnp.transpose(outcome, (1, 0, 2)).reshape(query_rows.shape[0], head_count * HEAD_DIM)


def shards(
    tokens,
    segment_ids,
    prefix_lengths,
    page_owner,
    slot_perm,
    ln_gain,
    ln_bias,
    qkv_weight,
    qkv_bias,
    dense_weight,
    dense_bias,
    fc1_weight,
    fc1_bias,
    fc2_weight,
    fc2_bias,
    prefix_cache,
    cache_pool,
):
    req_count = lax.axis_size("req")
    req_index = lax.axis_index("req")
    tok_rows = tokens.shape[0]
    prefix_count = prefix_cache.shape[0]
    head_cols = qkv_weight.shape[2]
    pool_count = slot_perm.shape[1]
    page_cap = pool_count // req_count
    gathered = lax.all_gather(tokens, "tensor", axis=1, tiled=True)
    normed = norm_rows(gathered.astype(jnp.float32), ln_gain, ln_bias)
    row_ids = jnp.arange(tok_rows, dtype=jnp.int32)
    places = req_index * tok_rows + row_ids
    labels = jnp.arange(prefix_lengths.shape[0], dtype=jnp.int32)
    label_count = labels.shape[0]
    beyond = tok_rows * req_count
    earliest_rows = jnp.min(
        jnp.where(segment_ids[:, None] == labels[None, :], places[:, None], beyond), axis=0
    )
    weight_rows = qkv_weight.shape[0]
    digit_cols = 128
    digits = jnp.concatenate([earliest_rows // 128, earliest_rows % 128]).astype(jnp.bfloat16)
    digits = jnp.pad(digits, (0, weight_rows * digit_cols - 2 * label_count)).reshape(
        weight_rows, digit_cols
    )
    qkv_local = qkv_weight.reshape(weight_rows, 3 * head_cols)
    fc1_cols = fc1_weight.shape[1]
    dense_cols = dense_weight.shape[0]
    fc2_cols = fc2_weight.shape[0]
    packed = jnp.concatenate([qkv_local, fc1_weight, dense_weight.T, fc2_weight.T, digits], axis=1)
    everything = lax.all_gather(packed, "req", axis=0, tiled=True)
    edges = [0]
    for width in (3 * head_cols, fc1_cols, dense_cols, fc2_cols, digit_cols):
        edges.append(edges[-1] + width)
    qkv_full, fc1_full, dense_full_t, fc2_full_t, digits_full = [
        everything[:, edges[i] : edges[i + 1]] for i in range(5)
    ]
    digit_table = digits_full.reshape(req_count, weight_rows * digit_cols)[:, : 2 * label_count]
    digit_table = digit_table.astype(jnp.int32)
    starts = jnp.min(digit_table[:, :label_count] * 128 + digit_table[:, label_count:], axis=0)

    def add_rows(portion):
        return jnp.dot(normed, portion, preferred_element_type=jnp.float32)

    projected = add_rows(qkv_full)
    lifted = add_rows(fc1_full)
    projected = (projected + qkv_bias.reshape(1, 3 * head_cols)).reshape(
        tok_rows, 3, head_cols // HEAD_DIM, HEAD_DIM
    )
    segment, position = label_rows(places, starts, prefix_lengths)
    queries = (
        rotate_heads(projected[:, 0], position).astype(jnp.bfloat16).reshape(tok_rows, head_cols)
    )
    new_keys = (
        rotate_heads(projected[:, 1], position).astype(jnp.bfloat16).reshape(tok_rows, head_cols)
    )
    new_values = projected[:, 2].astype(jnp.bfloat16).reshape(tok_rows, head_cols)
    key_value = jnp.stack([new_keys, new_values], axis=1)
    pages_here = tok_rows // PAGE
    page_width = PAGE * 2 * head_cols
    pages = key_value.reshape(pages_here, page_width)
    owners = page_owner[:, 0]
    onehot = (owners[:, None] == jnp.arange(req_count, dtype=jnp.int32)[None, :]).astype(jnp.int32)
    earlier = jnp.cumsum(onehot, axis=0) - onehot
    earlier_count = jnp.sum(earlier * onehot, axis=1)
    target = owners * page_cap + earlier_count
    selecting = (target[None, :] == jnp.arange(pool_count, dtype=jnp.int32)[:, None]).astype(
        jnp.bfloat16
    )
    outgoing = jnp.dot(selecting, pages, preferred_element_type=jnp.float32).astype(jnp.bfloat16)
    filled = jnp.sum(selecting, axis=1)
    flag_cols = 128
    flagged = jnp.concatenate(
        [outgoing, jnp.broadcast_to(filled[:, None], (pool_count, flag_cols)).astype(jnp.bfloat16)],
        axis=1,
    )
    arrived = lax.all_to_all(
        flagged.reshape(req_count, page_cap, page_width + flag_cols),
        "req",
        split_axis=0,
        concat_axis=0,
        tiled=True,
    ).reshape(pool_count, page_width + flag_cols)
    incoming = arrived[:, :page_width]
    incoming_filled = arrived[:, page_width]
    slot_ids = slot_perm[0]
    placing = (slot_ids[None, :] == jnp.arange(pool_count, dtype=jnp.int32)[:, None]) & (
        incoming_filled[None, :] > 0
    )
    written = jnp.dot(
        placing.astype(jnp.bfloat16), incoming, preferred_element_type=jnp.float32
    ).astype(jnp.bfloat16)
    written_mask = jnp.any(placing, axis=1)
    pool_pages = cache_pool.reshape(pool_count, page_width)
    new_pool = jnp.where(written_mask[:, None], written, pool_pages).reshape(cache_pool.shape)
    local_keys = jnp.concatenate([key_value, prefix_cache], axis=0)
    blocks = [local_keys]
    for shift_by in range(1, SPAN + 1):
        blocks.append(from_behind(local_keys, "req", shift_by))
    key_segs = []
    key_poss = []
    for step_back in range(SPAN + 1):
        block_id = req_index - step_back
        seg_new, pos_new = label_rows(block_id * tok_rows + row_ids, starts, prefix_lengths)
        seg_old, pos_old = prefix_rows(block_id, tok_rows, prefix_count, starts, prefix_lengths)
        key_segs.extend([seg_new, seg_old])
        key_poss.extend([pos_new, pos_old])
    key_segment = jnp.concatenate(key_segs)
    key_position = jnp.concatenate(key_poss)
    allowed = (key_segment[None, :] == segment[:, None]) & (
        key_position[None, :] <= position[:, None]
    )
    allowed = allowed & (
        (position[:, None] - key_position[None, :] < WINDOW) | (key_position[None, :] < SINKS)
    )
    all_keys = jnp.concatenate(blocks, axis=0)
    attended = head_attention(queries, all_keys[:, 0, :], all_keys[:, 1, :], allowed)
    hidden = jax.nn.gelu(lifted + fc1_bias, approximate=True).astype(jnp.bfloat16)
    contract_rows = (((1,), (1,)), ((), ()))
    attn_part = lax.dot_general(
        attended, dense_full_t, contract_rows, preferred_element_type=jnp.float32
    )
    mlp_part = lax.dot_general(
        hidden, fc2_full_t, contract_rows, preferred_element_type=jnp.float32
    )
    branches = attn_part + mlp_part
    summed = lax.psum_scatter(branches, "tensor", scatter_dimension=1, tiled=True)
    layer_out = (tokens.astype(jnp.float32) + summed + dense_bias + fc2_bias).astype(jnp.bfloat16)
    return (layer_out, new_pool)


def solution(mesh):
    placed = (
        P("req", "tensor"),
        P("req"),
        P(),
        P("req", None),
        P("req", None),
        P(),
        P(),
        P("req", None, "tensor"),
        P(None, "tensor"),
        P("tensor", "req"),
        P("tensor"),
        P("req", "tensor"),
        P("tensor"),
        P("tensor", "req"),
        P("tensor"),
        P("req", None, "tensor"),
        P("req", None, "tensor"),
    )
    return jax.shard_map(
        shards,
        mesh=mesh,
        in_specs=placed,
        out_specs=(P("req", "tensor"), P("req", None, "tensor")),
        check_vma=False,
    )
```

profile of v0, /device:TPU:6, one launch (start us, length us, event | category | flops | bytes accessed | tf_op | source)
XLA Modules:
  0.0 319.7 jit_solution(9198134115274271958)
XLA Ops:
  7.2 0.7 all-gather.3.cloned.1.call-update
  8.0 0.8 copy.50
  8.8 0.8 constant_dynamic-update-slice_fusion.2
  9.5 0.8 select_reduce_fusion.6
  10.4 0.7 constant_dynamic-update-slice_fusion.1
  11.1 0.8 bitcast_dynamic-update-slice_fusion
  11.9 0.7 copy-done.3
  12.7 0.7 add.197
  13.4 1.1 copy.42
  14.5 30.4 %all-gather.3.cloned.1.call-done = bf16[256,2048]{1,0:T(8,128)(2,1)} async-done(((bf16[256,256]{1,0:T(8,128)(2,1)}), bf16[256,2048]{1,0:T(8,128)(2,1)}) %all-gather.3.cloned.1.call-update) | async-done | bytes 1048592 | tf_op jit(solution)/shard_map/all_gather | solution.py:118
  45.0 1.5 convert_reduce_fusion
  46.5 1.6 fusion.25
  48.1 160.8 %all-gather.5.cloned.1.call-done = bf16[2048,2176]{1,0:T(8,128)(2,1)} async-done(((bf16[32,2176]{1,0:T(8,128)(2,1)}), bf16[2048,2176]{1,0:T(8,128)(2,1)}) %all-gather.5.cloned.1.call-update) | async-done | bytes 8912912 | tf_op jit(solution)/shard_map/all_gather | solution.py:139
  209.0 3.0 fusion.32
  212.4 0.7 slice-done
  213.4 0.7 fusion.84
  214.1 0.7 select_reduce_fusion.9
  214.8 0.7 reduce_or.36
  215.6 1.7 constant_dynamic-update-slice_fusion.14
  217.4 1.9 constant_dynamic-update-slice_fusion.8
  219.8 3.6 %collective-permute-start.1 = (bf16[512,2,256]{0,2,1:T(8,128)(2,1)S(1)}, bf16[512,2,256]{0,2,1:T(8,128)(2,1)S(1)}, u32[]{:S(2)}, u32[]{:S(2)}) collective-permute-start(bf16[512,2,256]{0,2,1:T(8,128)(2,1)S(1)} %pad_maximum_fusion.2), channel_id=1, source_target_pairs={{0,16},{8,24},{16,32},{24,40},{32,48},{40,56},{48,64},{56,72},{64,... | collective-permute-start | bytes 1572872 | tf_op jit(solution)/shard_map/ppermute | solution.py:18
  223.4 2.0 collective-permute-start
  225.5 1.8 constant_dynamic-update-slice_fusion.6
  227.4 5.3 %collective-permute-done.1 = bf16[512,2,256]{0,2,1:T(8,128)(2,1)S(1)} collective-permute-done((bf16[512,2,256]{0,2,1:T(8,128)(2,1)S(1)}, bf16[512,2,256]{0,2,1:T(8,128)(2,1)S(1)}, u32[]{:S(2)}, u32[]{:S(2)}) %collective-permute-start.1) | collective-permute-done | bytes 524320 | tf_op jit(solution)/shard_map/ppermute | solution.py:18
  232.7 5.6 %collective-permute-done = bf16[512,2,256]{0,2,1:T(8,128)(2,1)S(1)} collective-permute-done((bf16[512,2,256]{0,2,1:T(8,128)(2,1)S(1)}, bf16[512,2,256]{0,2,1:T(8,128)(2,1)S(1)}, u32[]{:S(2)}, u32[]{:S(2)}) %collective-permute-start) | collective-permute-done | bytes 524320 | tf_op jit(solution)/shard_map/ppermute | solution.py:18
  238.6 0.8 copy-done.4
  239.3 15.9 %while.11 = (s32[]{:T(128)}, bf16[4,256,64]{1,2,0:T(8,128)(2,1)S(1)}, s32[4]{0:T(128)S(1)}, bf16[256,256]{0,1:T(8,128)(2,1)S(1)}, bf16[1536,256]{0,1:T(8,128)(2,...) while((s32[]{:T(128)}, ...), condition=%wide.region_25.26_spmd.clone, body=%wide.region_22.25_spmd.clone.sunk | while | flops 112492032 | bytes 5240535 | solution.py:88
  240.6 0.9 fusion.95
  241.5 0.9 fusion.96
  242.4 0.9 fusion.97
  244.5 0.9 fusion.95
  245.4 0.9 fusion.96
  246.4 0.9 fusion.97
  248.5 0.9 fusion.95
  249.4 0.9 fusion.96
  250.3 0.9 fusion.97
  252.5 0.9 fusion.95
  253.4 0.9 fusion.96
  254.3 0.9 fusion.97
  255.2 0.6 copy-done.5
  255.9 1.8 fusion.38
  257.7 5.1 %convolution_add_fusion = f32[256,2048]{1,0:T(8,128)} fusion(f32[256,2048]{1,0:T(8,128)S(1)} %fusion.38, bf16[2048,2176]{1,0:T(8,128)(2,1)} %all-gather.5.cloned.1.call-done, f32[512]{0:T(512)S(1)} %copy-done.13, bf16[256,2048]{1,0:T(8,128)(2,1)S(1)} %copy-done, f32[2048]{0:T(1024)S(1)} %copy-done.11, f32[2048]{0:T(1024)S(1)} %copy-done.12, ...), kind=kOutput, calls=%fused_computation.23 | convolution fusion | flops 1078722560 | bytes 9457664 | tf_op jit(solution)/shard_map/dot_general | solution.py:231
  262.8 0.6 copy-done.6
  264.9 1.0 reshape.258
  265.9 12.5 %all-to-all-start = ((bf16[64,2,2176]{2,1,0:T(2,128)(2,1)}), bf16[64,2,2176]{2,1,0:T(2,128)(2,1)S(1)}, u32[]{:S(2)}, u32[]{:S(2)}) async-start(bf16[64,2,2176]{2,1,0:T(2,128)(2,1)} %reshape.258), calls=%async_computation.1 | async-start | bytes 1114112 | tf_op jit(solution)/shard_map/all_to_all | solution.py:185
  278.9 30.7 %all-to-all-done = bf16[64,2,2176]{2,1,0:T(2,128)(2,1)S(1)} async-done(((bf16[64,2,2176]{2,1,0:T(2,128)(2,1)}), bf16[64,2,2176]{2,1,0:T(2,128)(2,1)S(1)}, u32[]{:S(2)}, u32[]{:S(2)}) %all-to-all-start) | async-done | bytes 557088 | tf_op jit(solution)/shard_map/all_to_all | solution.py:185
  310.3 1.2 reshape.261
  311.5 1.6 add_convert_fusion
  (92 shorter events, 6.7 us)
Async XLA Ops:
  7.2 201.8 %copy-start.11 = (f32[2048]{0:T(1024)S(1)}, f32[2048]{0:T(1024)}, u32[]{:S(2)}) copy-start(f32[2048]{0:T(1024)} %param.25) | copy-start | bytes 24580
  7.2 201.8 %copy-start.12 = (f32[2048]{0:T(1024)S(1)}, f32[2048]{0:T(1024)}, u32[]{:S(2)}) copy-start(f32[2048]{0:T(1024)} %param.24) | copy-start | bytes 24580
  7.2 37.8 %all-gather.3.cloned.1.call-start = ((), (), s32[]{:S(2)}) async-start(), calls=%async_computation.2 | async-start | bytes 1179648 | tf_op jit(solution)/shard_map/all_gather | solution.py:118
  7.9 201.0 %all-gather.5.cloned.1.call-start = ((), (), s32[]{:S(2)}) async-start(), calls=%async_computation.3 | async-start | bytes 9052160 | tf_op jit(solution)/shard_map/all_gather | solution.py:139
  11.9 0.7 copy-start.3
  12.6 298.9 %reduce-scatter.2.cloned.1.call-start = ((), (), s32[]{:S(2)}) async-start(), calls=%async_computation.4 | async-start | bytes 2359296 | tf_op jit(solution)/shard_map/reduce_scatter | solution.py:235
  45.0 164.0 %copy-start = (bf16[256,2048]{1,0:T(8,128)(2,1)S(1)}, bf16[256,2048]{1,0:T(8,128)(2,1)}, u32[]{:S(2)}) copy-start(bf16[256,2048]{1,0:T(8,128)(2,1)} %all-gather.3.cloned.1.call-done) | copy-start | bytes 3145732
  212.0 1.0 slice-start
  212.3 1.8 copy-start.7
  219.8 12.9 %collective-permute-start.1 = (bf16[512,2,256]{0,2,1:T(8,128)(2,1)S(1)}, bf16[512,2,256]{0,2,1:T(8,128)(2,1)S(1)}, u32[]{:S(2)}, u32[]{:S(2)}) collective-permute-start(bf16[512,2,256]{0,2,1:T(8,128)(2,1)S(1)} %pad_maximum_fusion.2), channel_id=1, source_target_pairs={{0,16},{8,24},{16,32},{24,40},{32,48},{40,56},{48,64},{56,72},{64,... | collective-permute-start | bytes 1572872 | tf_op jit(solution)/shard_map/ppermute | solution.py:18
  223.4 14.9 %collective-permute-start = (bf16[512,2,256]{0,2,1:T(8,128)(2,1)S(1)}, bf16[512,2,256]{0,2,1:T(8,128)(2,1)S(1)}, u32[]{:S(2)}, u32[]{:S(2)}) collective-permute-start(bf16[512,2,256]{0,2,1:T(8,128)(2,1)S(1)} %pad_maximum_fusion.2), channel_id=1, source_target_pairs={{0,8},{8,16},{16,24},{24,32},{32,40},{40,48},{48,56},{56,64},{64,7... | collective-permute-start | bytes 1572872 | tf_op jit(solution)/shard_map/ppermute | solution.py:18
  238.4 0.9 copy-start.4
  255.2 0.7 copy-start.5
  255.2 2.4 copy-start.13
  262.8 0.7 copy-start.6
  264.3 14.1 %copy-start.1 = (bf16[512,2,256]{2,1,0:T(2,128)(2,1)S(1)}, bf16[512,2,256]{2,1,0:T(2,128)(2,1)}, u32[]{:S(2)}) copy-start(bf16[512,2,256]{2,1,0:T(2,128)(2,1)} %param.35) | copy-start | bytes 1572868
  264.9 45.0 %copy-start.10 = (s32[1,128]{1,0:T(1,128)S(1)}, s32[1,128]{1,0:T(1,128)}, u32[]{:S(2)}) copy-start(s32[1,128]{1,0:T(1,128)} %param.23) | copy-start | bytes 1540
  265.9 43.7 %all-to-all-start = ((bf16[64,2,2176]{2,1,0:T(2,128)(2,1)}), bf16[64,2,2176]{2,1,0:T(2,128)(2,1)S(1)}, u32[]{:S(2)}, u32[]{:S(2)}) async-start(bf16[64,2,2176]{2,1,0:T(2,128)(2,1)} %reshape.258), calls=%async_computation.1 | async-start | bytes 1114112 | tf_op jit(solution)/shard_map/all_to_all | solution.py:185
  278.8 32.7 %copy-start.2 = (bf16[256,256]{1,0:T(8,128)(2,1)S(1)}, bf16[256,256]{1,0:T(8,128)(2,1)}, u32[]{:S(2)}) copy-start(bf16[256,256]{1,0:T(8,128)(2,1)} %param.19) | copy-start | bytes 393220
  278.8 32.7 %copy-start.8 = (f32[256]{0:T(256)S(1)}, f32[256]{0:T(256)}, u32[]{:S(2)}) copy-start(f32[256]{0:T(256)} %param.33) | copy-start | bytes 3076
  278.9 32.7 %copy-start.9 = (f32[256]{0:T(256)S(1)}, f32[256]{0:T(256)}, u32[]{:S(2)}) copy-start(f32[256]{0:T(256)} %param.29) | copy-start | bytes 3076
Sparse Core Ops, SparseCore 0:
  10.1 34.7 all-gather.2
  48.5 160.4 all-gather.4
  262.9 36.6 reduce-scatter.1
where the time goes:
time: 321 us; the launch traced here: 320 us
  waiting for transfers between devices  234 us (73%)
  other arithmetic  18.5 us (6%)
  starting transfers between devices  18.3 us (6%)
  matrix products  17.8 us (6%)
  local copies, waits for them, and re-layouts  14.5 us (5%)
  between operations  14.3 us (4%)
    all_gather x1, waiting for transfers between devices, shards(): everything = lax.all_gather(packed, 'req', axis=0, tiled=True)  161 us
    all_to_all x1, waiting for transfers between devices, shards(): lax.all_to_all(flagged.reshape(req_count, page_cap, page_width + flag_col...  30.7 us
    all_gather x1, waiting for transfers between devices, shards(): gathered = lax.all_gather(tokens, 'tensor', axis=1, tiled=True)  30.4 us
    all_to_all x1, starting transfers between devices, shards(): lax.all_to_all(flagged.reshape(req_count, page_cap, page_width + flag_col...  12.5 us
    ppermute x2, waiting for transfers between devices, from_behind(): lax.ppermute(value, axis, [(source, source + steps) for source in range(l...  10.9 us
  transfers between devices with their start and end apart: 6, of which 5 were waited for; matrix products, arithmetic and copies ran while one was open for 5% of the time, Pallas kernels for 0%

commit v1 on v0

--- a/solution.py
+++ b/solution.py
@@ -115,7 +115,14 @@
     head_cols = qkv_weight.shape[2]
     pool_count = slot_perm.shape[1]
     page_cap = pool_count // req_count
-    gathered = lax.all_gather(tokens, "tensor", axis=1, tiled=True)
+    ring = [tokens]
+    for hop in range(7):
+        ring.append(lax.ppermute(ring[-1], "tensor", [(dev, (dev + 1) % 8) for dev in range(8)]))
+    gathered = jnp.roll(
+        jnp.concatenate(ring[::-1], axis=1),
+        (lax.axis_index("tensor") + 1) * ring[0].shape[1],
+        axis=1,
+    )
     normed = norm_rows(gathered.astype(jnp.float32), ln_gain, ln_bias)
     row_ids = jnp.arange(tok_rows, dtype=jnp.int32)
     places = req_index * tok_rows + row_ids

time: 321 us -> 300 us (0.935)
  waiting for transfers between devices: 234 us -> 174 us
  starting transfers between devices: 18.3 us -> 44.9 us
  matrix products: 17.8 us -> 24.5 us
  local copies, waits for them, and re-layouts: 14.5 us -> 18.6 us
    all_gather x1, waiting for transfers between devices: 161 us -> 124 us  [shards(): everything = lax.all_gather(packed, 'req', axis=0, tiled=True)]
    all_gather x1 -> x0, waiting for transfers between devices: 30.4 us -> none  [shards(): gathered = lax.all_gather(tokens, 'tensor', axis=1, tiled=True)]
    ppermute x0 -> x7, starting transfers between devices: none -> 26.6 us  [shards(): lax.ppermute(ring[-1], 'tensor', [(dev, (dev + 1) % 8) for dev in range(8)])]
    ppermute x0 -> x7, waiting for transfers between devices: none -> 8.92 us  [shards(): lax.ppermute(ring[-1], 'tensor', [(dev, (dev + 1) % 8) for dev in range(8)])]
    dot_general x4, matrix products: 3.56 us -> 7.33 us  [one_head(): lax.dot_general(query_cols, key_cols, (((1,), (1,)), ((), ())), preferred...]
  transfers between devices with their start and end apart: 6 -> 12, of which waited for: 5 -> 10; matrix products, arithmetic and copies ran while one was open for 5% -> 4% of each run, Pallas kernels for 0% -> 0%
where the time goes in v1:
time: 300 us; the launch traced here: 299 us
  waiting for transfers between devices  174 us (58%)
  starting transfers between devices  44.9 us (15%)
  matrix products  24.5 us (8%)
  other arithmetic  20.3 us (7%)
  local copies, waits for them, and re-layouts  18.6 us (6%)
  between operations  14.7 us (5%)
    all_gather x1, waiting for transfers between devices, shards(): everything = lax.all_gather(packed, 'req', axis=0, tiled=True)  124 us
    all_to_all x1, waiting for transfers between devices, shards(): lax.all_to_all(flagged.reshape(req_count, page_cap, page_width + flag_col...  30.7 us
    ppermute x7, starting transfers between devices, shards(): lax.ppermute(ring[-1], 'tensor', [(dev, (dev + 1) % 8) for dev in range(8)])  26.6 us
    all_to_all x1, starting transfers between devices, shards(): lax.all_to_all(flagged.reshape(req_count, page_cap, page_width + flag_col...  12.5 us
    ppermute x2, waiting for transfers between devices, from_behind(): lax.ppermute(value, axis, [(source, source + steps) for source in range(l...  9.56 us
    ppermute x7, waiting for transfers between devices, shards(): lax.ppermute(ring[-1], 'tensor', [(dev, (dev + 1) % 8) for dev in range(8)])  8.92 us
    dot_general x4, matrix products, one_head(): lax.dot_general(query_cols, key_cols, (((1,), (1,)), ((), ())), preferred...  7.33 us
    unnamed x72, local copies, waits for them, and re-layouts  6.13 us
  transfers between devices with their start and end apart: 12, of which 10 were waited for; matrix products, arithmetic and copies ran while one was open for 4% of the time, Pallas kernels for 0%

profile of v1, /device:TPU:6, one launch (start us, length us, event | category | flops | bytes accessed | tf_op | source)
XLA Modules:
  0.0 299.3 jit_solution(304602839520966658)
XLA Ops:
  7.2 0.8 copy.50
  12.0 4.6 %collective-permute-done = bf16[256,256]{1,0:T(8,128)(2,1)S(1)} collective-permute-done((bf16[256,256]{1,0:T(8,128)(2,1)}, bf16[256,256]{1,0:T(8,128)(2,1)S(1)}, u32[]{:S(2)}, u32[]{:S(2)}) %collective-permute-start) | collective-permute-done | bytes 131104 | tf_op jit(solution)/shard_map/ppermute | solution.py:120
  16.6 3.6 %collective-permute-start.1 = (bf16[256,256]{1,0:T(8,128)(2,1)S(1)}, bf16[256,256]{1,0:T(8,128)(2,1)S(1)}, u32[]{:S(2)}, u32[]{:S(2)}) collective-permute-start(bf16[256,256]{1,0:T(8,128)(2,1)S(1)} %collective-permute-done), channel_id=1, source_target_pairs={{0,1},{1,2},{2,3},{3,4},{4,5},{5,6},{6,7},{7,0},{8,9},{9,10},{10,1... | collective-permute-start | bytes 393224 | tf_op jit(solution)/shard_map/ppermute | solution.py:120
  20.2 1.0 collective-permute-done.1
  21.2 4.5 %collective-permute-start.2 = (bf16[256,256]{1,0:T(8,128)(2,1)S(1)}, bf16[256,256]{1,0:T(8,128)(2,1)S(1)}, u32[]{:S(2)}, u32[]{:S(2)}) collective-permute-start(bf16[256,256]{1,0:T(8,128)(2,1)S(1)} %collective-permute-done.1), channel_id=1, source_target_pairs={{0,1},{1,2},{2,3},{3,4},{4,5},{5,6},{6,7},{7,0},{8,9},{9,10},{10,1... | collective-permute-start | bytes 393224 | tf_op jit(solution)/shard_map/ppermute | solution.py:120
  25.7 1.0 collective-permute-done.2
  26.7 4.6 %collective-permute-start.3 = (bf16[256,256]{1,0:T(8,128)(2,1)S(1)}, bf16[256,256]{1,0:T(8,128)(2,1)S(1)}, u32[]{:S(2)}, u32[]{:S(2)}) collective-permute-start(bf16[256,256]{1,0:T(8,128)(2,1)S(1)} %collective-permute-done.2), channel_id=1, source_target_pairs={{0,1},{1,2},{2,3},{3,4},{4,5},{5,6},{6,7},{7,0},{8,9},{9,10},{10,1... | collective-permute-start | bytes 393224 | tf_op jit(solution)/shard_map/ppermute | solution.py:120
  31.3 1.0 collective-permute-done.3
  32.3 4.6 %collective-permute-start.4 = (bf16[256,256]{1,0:T(8,128)(2,1)S(1)}, bf16[256,256]{1,0:T(8,128)(2,1)S(1)}, u32[]{:S(2)}, u32[]{:S(2)}) collective-permute-start(bf16[256,256]{1,0:T(8,128)(2,1)S(1)} %collective-permute-done.3), channel_id=1, source_target_pairs={{0,1},{1,2},{2,3},{3,4},{4,5},{5,6},{6,7},{7,0},{8,9},{9,10},{10,1... | collective-permute-start | bytes 393224 | tf_op jit(solution)/shard_map/ppermute | solution.py:120
  36.9 1.0 collective-permute-done.4
  37.9 4.6 %collective-permute-start.5 = (bf16[256,256]{1,0:T(8,128)(2,1)S(1)}, bf16[256,256]{1,0:T(8,128)(2,1)S(1)}, u32[]{:S(2)}, u32[]{:S(2)}) collective-permute-start(bf16[256,256]{1,0:T(8,128)(2,1)S(1)} %collective-permute-done.4), channel_id=1, source_target_pairs={{0,1},{1,2},{2,3},{3,4},{4,5},{5,6},{6,7},{7,0},{8,9},{9,10},{10,1... | collective-permute-start | bytes 393224 | tf_op jit(solution)/shard_map/ppermute | solution.py:120
  43.5 4.6 %collective-permute-start.6 = (bf16[256,256]{1,0:T(8,128)(2,1)S(1)}, bf16[256,256]{1,0:T(8,128)(2,1)S(1)}, u32[]{:S(2)}, u32[]{:S(2)}) collective-permute-start(bf16[256,256]{1,0:T(8,128)(2,1)S(1)} %collective-permute-done.5), channel_id=1, source_target_pairs={{0,1},{1,2},{2,3},{3,4},{4,5},{5,6},{6,7},{7,0},{8,9},{9,10},{10,1... | collective-permute-start | bytes 393224 | tf_op jit(solution)/shard_map/ppermute | solution.py:120
  48.8 1.1 copy.42
  51.0 124.3 %all-gather.2.cloned.1.call-done = bf16[2048,2176]{1,0:T(8,128)(2,1)} async-done(((bf16[32,2176]{1,0:T(8,128)(2,1)}), bf16[2048,2176]{1,0:T(8,128)(2,1)}) %all-gather.2.cloned.1.call-update) | async-done | bytes 8912912 | tf_op jit(solution)/shard_map/all_gather | solution.py:146
  175.3 4.0 %fusion.32 = f32[256,768]{1,0:T(8,128)} fusion(bf16[2048,2176]{1,0:T(8,128)(2,1)} %all-gather.2.cloned.1.call-done, f32[768]{0:T(1024)S(1)} %add.213, f32[2048]{0:T(1024)S(1)} %copy-done.20, f32[2048]{0:T(1024)S(1)} %copy-done.22, f32[256]{0:T(256)S(1)} %add_rsqrt_fusion, f32[256]{0:T(256)S(1)} %broadcast_multiply_fusion, ...), kind=kOutput, calls=%fused_computation.39 | convolution fusion | flops 808648704 | bytes 5003268 | tf_op jit(solution)/shard_map/dot_general | solution.py:158
  179.3 1.4 copy.40
  182.2 1.1 slice.97
  183.3 1.0 reshape.255
  187.4 1.8 constant_dynamic-update-slice_fusion.31
  189.3 1.9 constant_dynamic-update-slice_fusion.25
  191.9 0.8 multiply_cosine_fusion
  192.7 0.9 subtract_convert_fusion
  193.7 3.6 %collective-permute-start.8 = (bf16[512,2,256]{0,2,1:T(8,128)(2,1)S(1)}, bf16[512,2,256]{0,2,1:T(8,128)(2,1)S(1)}, u32[]{:S(2)}, u32[]{:S(2)}) collective-permute-start(bf16[512,2,256]{0,2,1:T(8,128)(2,1)S(1)} %pad_maximum_fusion.2), channel_id=1, source_target_pairs={{0,16},{8,24},{16,32},{24,40},{32,48},{40,56},{48,64},{56,72},{64,... | collective-permute-start | bytes 1572872 | tf_op jit(solution)/shard_map/ppermute | solution.py:18
  197.3 2.0 collective-permute-start.7
  199.4 1.9 constant_dynamic-update-slice_fusion.23
  202.6 3.9 %collective-permute-done.8 = bf16[512,2,256]{0,2,1:T(8,128)(2,1)S(1)} collective-permute-done((bf16[512,2,256]{0,2,1:T(8,128)(2,1)S(1)}, bf16[512,2,256]{0,2,1:T(8,128)(2,1)S(1)}, u32[]{:S(2)}, u32[]{:S(2)}) %collective-permute-start.8) | collective-permute-done | bytes 524320 | tf_op jit(solution)/shard_map/ppermute | solution.py:18
  206.6 5.6 %collective-permute-done.7 = bf16[512,2,256]{0,2,1:T(8,128)(2,1)S(1)} collective-permute-done((bf16[512,2,256]{0,2,1:T(8,128)(2,1)S(1)}, bf16[512,2,256]{0,2,1:T(8,128)(2,1)S(1)}, u32[]{:S(2)}, u32[]{:S(2)}) %collective-permute-start.7) | collective-permute-done | bytes 524320 | tf_op jit(solution)/shard_map/ppermute | solution.py:18
  212.4 1.1 slice_bitcast_fusion
  213.4 19.6 %while.11 = (s32[]{:T(128)}, bf16[4,256,64]{1,2,0:T(8,128)(2,1)S(1)}, s32[4]{0:T(128)S(1)}, bf16[256,256]{0,1:T(8,128)(2,1)}, bf16[1536,256]{0,1:T(8,128)(2,1)},...) while((s32[]{:T(128)}, ...), condition=%wide.region_25.26_spmd.clone, body=%wide.region_22.25_spmd.clone.sunk | while | flops 112492032 | bytes 5235927 | solution.py:88
  214.7 1.8 fusion.95
  216.5 0.9 fusion.96
  217.5 0.9 fusion.97
  219.6 1.8 fusion.95
  221.4 0.9 fusion.96
  222.4 0.9 fusion.97
  224.5 1.8 fusion.95
  226.4 0.9 fusion.96
  227.3 0.9 fusion.97
  229.4 1.8 fusion.95
  231.3 0.9 fusion.96
  232.2 0.9 fusion.97
  233.2 3.1 %fusion.38 = f32[256,2048]{1,0:T(8,128)} fusion(bf16[256,256]{0,1:T(8,128)(2,1)S(1)} %bitcast.50, bf16[2048,2176]{1,0:T(8,128)(2,1)} %all-gather.2.cloned.1.call-done), kind=kOutput, calls=%fused_computation.41 | convolution fusion | flops 268435456 | bytes 3276800 | tf_op jit(solution)/shard_map/dot_general | solution.py:235
  236.3 5.8 %convolution_add_fusion = f32[256,2048]{1,0:T(8,128)} fusion(f32[256,2048]{1,0:T(8,128)} %fusion.38, bf16[2048,2176]{1,0:T(8,128)(2,1)} %all-gather.2.cloned.1.call-done, f32[512]{0:T(512)S(1)} %copy-done.24, f32[2048]{0:T(1024)S(1)} %copy-done.21, f32[2048]{0:T(1024)S(1)} %copy-done.23, f32[256]{0:T(256)S(1)} %copy-done.18, f32[256]{0:T(256)S(1)} %copy-done.12, ...), kind=kOutput, calls=%fused_computation.23 | convolution fusion | flops 1078722560 | bytes 9457668 | tf_op jit(solution)/shard_map/dot_general | solution.py:238
  244.2 1.0 reshape.258
  245.2 12.5 %all-to-all-start = ((bf16[64,2,2176]{2,1,0:T(2,128)(2,1)}), bf16[64,2,2176]{2,1,0:T(2,128)(2,1)S(1)}, u32[]{:S(2)}, u32[]{:S(2)}) async-start(bf16[64,2,2176]{2,1,0:T(2,128)(2,1)} %reshape.258), calls=%async_computation.1 | async-start | bytes 1114112 | tf_op jit(solution)/shard_map/all_to_all | solution.py:192
  258.2 30.7 %all-to-all-done = bf16[64,2,2176]{2,1,0:T(2,128)(2,1)S(1)} async-done(((bf16[64,2,2176]{2,1,0:T(2,128)(2,1)}), bf16[64,2,2176]{2,1,0:T(2,128)(2,1)S(1)}, u32[]{:S(2)}, u32[]{:S(2)}) %all-to-all-start) | async-done | bytes 557088 | tf_op jit(solution)/shard_map/all_to_all | solution.py:192
  289.6 1.2 reshape.261
  290.8 1.6 add_convert_fusion
  (140 shorter events, 18.7 us)
Async XLA Ops:
  7.2 42.9 %copy-start = (bf16[256,256]{1,0:T(8,128)(2,1)S(1)}, bf16[256,256]{1,0:T(8,128)(2,1)}, u32[]{:S(2)}) copy-start(bf16[256,256]{1,0:T(8,128)(2,1)} %param.19) | copy-start | bytes 393220
  7.2 168.1 %all-gather.2.cloned.1.call-start = ((), (), s32[]{:S(2)}) async-start(), calls=%async_computation.2 | async-start | bytes 9052160 | tf_op jit(solution)/shard_map/all_gather | solution.py:146
  11.2 0.7 copy-start.4
  11.9 278.9 %reduce-scatter.2.cloned.1.call-start = ((), (), s32[]{:S(2)}) async-start(), calls=%async_computation.3 | async-start | bytes 2359296 | tf_op jit(solution)/shard_map/reduce_scatter | solution.py:242
  11.9 4.6 %collective-permute-start = (bf16[256,256]{1,0:T(8,128)(2,1)}, bf16[256,256]{1,0:T(8,128)(2,1)S(1)}, u32[]{:S(2)}, u32[]{:S(2)}) collective-permute-start(bf16[256,256]{1,0:T(8,128)(2,1)} %param.19), channel_id=1, source_target_pairs={{0,1},{1,2},{2,3},{3,4},{4,5},{5,6},{6,7},{7,0},{8,9},{9,10},{10,1... | collective-permute-start | bytes 393224 | tf_op jit(solution)/shard_map/ppermute | solution.py:120
  16.6 4.6 %collective-permute-start.1 = (bf16[256,256]{1,0:T(8,128)(2,1)S(1)}, bf16[256,256]{1,0:T(8,128)(2,1)S(1)}, u32[]{:S(2)}, u32[]{:S(2)}) collective-permute-start(bf16[256,256]{1,0:T(8,128)(2,1)S(1)} %collective-permute-done), channel_id=1, source_target_pairs={{0,1},{1,2},{2,3},{3,4},{4,5},{5,6},{6,7},{7,0},{8,9},{9,10},{10,1... | collective-permute-start | bytes 393224 | tf_op jit(solution)/shard_map/ppermute | solution.py:120
  21.2 5.5 %collective-permute-start.2 = (bf16[256,256]{1,0:T(8,128)(2,1)S(1)}, bf16[256,256]{1,0:T(8,128)(2,1)S(1)}, u32[]{:S(2)}, u32[]{:S(2)}) collective-permute-start(bf16[256,256]{1,0:T(8,128)(2,1)S(1)} %collective-permute-done.1), channel_id=1, source_target_pairs={{0,1},{1,2},{2,3},{3,4},{4,5},{5,6},{6,7},{7,0},{8,9},{9,10},{10,1... | collective-permute-start | bytes 393224 | tf_op jit(solution)/shard_map/ppermute | solution.py:120
  26.7 5.6 %collective-permute-start.3 = (bf16[256,256]{1,0:T(8,128)(2,1)S(1)}, bf16[256,256]{1,0:T(8,128)(2,1)S(1)}, u32[]{:S(2)}, u32[]{:S(2)}) collective-permute-start(bf16[256,256]{1,0:T(8,128)(2,1)S(1)} %collective-permute-done.2), channel_id=1, source_target_pairs={{0,1},{1,2},{2,3},{3,4},{4,5},{5,6},{6,7},{7,0},{8,9},{9,10},{10,1... | collective-permute-start | bytes 393224 | tf_op jit(solution)/shard_map/ppermute | solution.py:120
  32.3 5.6 %collective-permute-start.4 = (bf16[256,256]{1,0:T(8,128)(2,1)S(1)}, bf16[256,256]{1,0:T(8,128)(2,1)S(1)}, u32[]{:S(2)}, u32[]{:S(2)}) collective-permute-start(bf16[256,256]{1,0:T(8,128)(2,1)S(1)} %collective-permute-done.3), channel_id=1, source_target_pairs={{0,1},{1,2},{2,3},{3,4},{4,5},{5,6},{6,7},{7,0},{8,9},{9,10},{10,1... | collective-permute-start | bytes 393224 | tf_op jit(solution)/shard_map/ppermute | solution.py:120
  37.9 5.6 %collective-permute-start.5 = (bf16[256,256]{1,0:T(8,128)(2,1)S(1)}, bf16[256,256]{1,0:T(8,128)(2,1)S(1)}, u32[]{:S(2)}, u32[]{:S(2)}) collective-permute-start(bf16[256,256]{1,0:T(8,128)(2,1)S(1)} %collective-permute-done.4), channel_id=1, source_target_pairs={{0,1},{1,2},{2,3},{3,4},{4,5},{5,6},{6,7},{7,0},{8,9},{9,10},{10,1... | collective-permute-start | bytes 393224 | tf_op jit(solution)/shard_map/ppermute | solution.py:120
  43.5 6.4 %collective-permute-start.6 = (bf16[256,256]{1,0:T(8,128)(2,1)S(1)}, bf16[256,256]{1,0:T(8,128)(2,1)S(1)}, u32[]{:S(2)}, u32[]{:S(2)}) collective-permute-start(bf16[256,256]{1,0:T(8,128)(2,1)S(1)} %collective-permute-done.5), channel_id=1, source_target_pairs={{0,1},{1,2},{2,3},{3,4},{4,5},{5,6},{6,7},{7,0},{8,9},{9,10},{10,1... | collective-permute-start | bytes 393224 | tf_op jit(solution)/shard_map/ppermute | solution.py:120
  50.1 125.2 %copy-start.20 = (f32[2048]{0:T(1024)S(1)}, f32[2048]{0:T(1024)}, u32[]{:S(2)}) copy-start(f32[2048]{0:T(1024)} %param.25) | copy-start | bytes 24580
  50.1 125.2 %copy-start.22 = (f32[2048]{0:T(1024)S(1)}, f32[2048]{0:T(1024)}, u32[]{:S(2)}) copy-start(f32[2048]{0:T(1024)} %param.24) | copy-start | bytes 24580
  50.5 128.8 %copy-start.11 = (f32[256]{0:T(256)}, f32[256]{0:T(256)S(1)}, u32[]{:S(2)}) copy-start(f32[256]{0:T(256)S(1)} %broadcast_multiply_fusion) | copy-start | bytes 3076
  51.0 128.3 %copy-start.17 = (f32[256]{0:T(256)}, f32[256]{0:T(256)S(1)}, u32[]{:S(2)}) copy-start(f32[256]{0:T(256)S(1)} %add_rsqrt_fusion) | copy-start | bytes 3076
  180.7 5.1 %copy-start.14 = (s32[43]{0:T(128)S(1)}, s32[43]{0:T(128)}, u32[]{:S(2)}) copy-start(s32[43]{0:T(128)} %param.21) | copy-start | bytes 520
  181.5 0.7 copy-start.2
  181.5 10.4 %copy-start.1 = (f32[256,4,64]{0,2,1:T(8,128)S(1)}, f32[256,4,64]{0,2,1:T(8,128)}, u32[]{:S(2)}) copy-start(f32[256,4,64]{0,2,1:T(8,128)} %get-tuple-element.162) | copy-start | bytes 786436
  187.4 4.0 %copy-start.7 = (s32[256]{0:T(256)}, s32[256]{0:T(256)S(1)}, u32[]{:S(2)}) copy-start(s32[256]{0:T(256)S(1)} %get-tuple-element.255) | copy-start | bytes 3076
  191.3 0.5 copy-start.9
  193.7 12.9 %collective-permute-start.8 = (bf16[512,2,256]{0,2,1:T(8,128)(2,1)S(1)}, bf16[512,2,256]{0,2,1:T(8,128)(2,1)S(1)}, u32[]{:S(2)}, u32[]{:S(2)}) collective-permute-start(bf16[512,2,256]{0,2,1:T(8,128)(2,1)S(1)} %pad_maximum_fusion.2), channel_id=1, source_target_pairs={{0,16},{8,24},{16,32},{24,40},{32,48},{40,56},{48,64},{56,72},{64,... | collective-permute-start | bytes 1572872 | tf_op jit(solution)/shard_map/ppermute | solution.py:18
  197.3 14.9 %collective-permute-start.7 = (bf16[512,2,256]{0,2,1:T(8,128)(2,1)S(1)}, bf16[512,2,256]{0,2,1:T(8,128)(2,1)S(1)}, u32[]{:S(2)}, u32[]{:S(2)}) collective-permute-start(bf16[512,2,256]{0,2,1:T(8,128)(2,1)S(1)} %pad_maximum_fusion.2), channel_id=1, source_target_pairs={{0,8},{8,16},{16,24},{24,32},{32,40},{40,48},{48,56},{56,64},{64,7... | collective-permute-start | bytes 1572872 | tf_op jit(solution)/shard_map/ppermute | solution.py:18
  212.3 1.1 copy-start.5
  212.3 1.1 copy-start.6
  212.3 1.1 copy-start.8
  212.3 1.1 copy-start.10
  233.1 3.2 %copy-start.12 = (f32[256]{0:T(256)S(1)}, f32[256]{0:T(256)}, u32[]{:S(2)}) copy-start(f32[256]{0:T(256)} %copy-done.11) | copy-start | bytes 3076
  233.1 3.1 %copy-start.18 = (f32[256]{0:T(256)S(1)}, f32[256]{0:T(256)}, u32[]{:S(2)}) copy-start(f32[256]{0:T(256)} %copy-done.17) | copy-start | bytes 3076
  233.1 3.1 %copy-start.21 = (f32[2048]{0:T(1024)S(1)}, f32[2048]{0:T(1024)}, u32[]{:S(2)}) copy-start(f32[2048]{0:T(1024)} %param.25) | copy-start | bytes 24580
  233.1 3.1 %copy-start.23 = (f32[2048]{0:T(1024)S(1)}, f32[2048]{0:T(1024)}, u32[]{:S(2)}) copy-start(f32[2048]{0:T(1024)} %param.24) | copy-start | bytes 24580
  233.1 3.1 %copy-start.24 = (f32[512]{0:T(512)S(1)}, f32[512]{0:T(512)}, u32[]{:S(2)}) copy-start(f32[512]{0:T(512)} %param.31) | copy-start | bytes 6148
  242.1 0.7 copy-start.13
  243.6 14.1 %copy-start.3 = (bf16[512,2,256]{2,1,0:T(2,128)(2,1)S(1)}, bf16[512,2,256]{2,1,0:T(2,128)(2,1)}, u32[]{:S(2)}) copy-start(bf16[512,2,256]{2,1,0:T(2,128)(2,1)} %param.35) | copy-start | bytes 1572868
  244.2 45.0 %copy-start.19 = (s32[1,128]{1,0:T(1,128)S(1)}, s32[1,128]{1,0:T(1,128)}, u32[]{:S(2)}) copy-start(s32[1,128]{1,0:T(1,128)} %param.23) | copy-start | bytes 1540
  245.2 43.7 %all-to-all-start = ((bf16[64,2,2176]{2,1,0:T(2,128)(2,1)}), bf16[64,2,2176]{2,1,0:T(2,128)(2,1)S(1)}, u32[]{:S(2)}, u32[]{:S(2)}) async-start(bf16[64,2,2176]{2,1,0:T(2,128)(2,1)} %reshape.258), calls=%async_computation.1 | async-start | bytes 1114112 | tf_op jit(solution)/shard_map/all_to_all | solution.py:192
  258.2 32.6 %copy-start.15 = (f32[256]{0:T(256)S(1)}, f32[256]{0:T(256)}, u32[]{:S(2)}) copy-start(f32[256]{0:T(256)} %param.33) | copy-start | bytes 3076
  258.2 32.6 %copy-start.16 = (f32[256]{0:T(256)S(1)}, f32[256]{0:T(256)}, u32[]{:S(2)}) copy-start(f32[256]{0:T(256)} %param.29) | copy-start | bytes 3076
Sparse Core Ops, SparseCore 0:
  12.0 163.2 all-gather.1
  242.2 36.6 reduce-scatter.1
